TPU v7x, 256 devices: a whole 4x4x8 slice. The times are simulated.
256 devices in a mesh: ctx: 64 (over y, z, core), head: 4 (over x).
Axes of the slice: x: 4, y: 4, z: 8, core: 2. Of those that a mesh axis runs over, the one named last changes fastest.
Arguments:
- query_in: bfloat16 [8192, 2048], P('ctx', 'head'), may hold values from -6 to 6
- key_in: bfloat16 [8192, 2048], P('ctx', 'head'), may hold values from -6 to 6
- value_in: bfloat16 [8192, 4096], P('ctx', 'head'), may hold values from -6 to 6
- gate_in: bfloat16 [8192, 4096], P('ctx', 'head'), may hold values from -6 to 6
- conv_query: float32 [4, 2048], P(None, 'head'), may hold values from -3 to 3
- conv_key: float32 [4, 2048], P(None, 'head'), may hold values from -3 to 3
- conv_value: float32 [4, 4096], P(None, 'head'), may hold values from -3 to 3
- decay_in: float32 [32, 8192], P('head', 'ctx'), may hold values from -14 to 0.1
- beta_in: float32 [32, 8192], P('head', 'ctx'), may hold values from -2.5 to -1.5
- norm_gain: float32 [128], replicated, may hold values from 0.5 to 1.5
- doc_lengths: int32 [128], replicated, may hold values from 1 to 2048, 8192 in all
- out_weight: bfloat16 [4096, 2048], P('head'), may hold values from -0.09375 to 0.09375
Outputs:
- projected: bfloat16 [2048, 8192], P('head', 'ctx')
Inputs may be any that keep to these rules, and one draw needn't show every extreme that they name: `doc_lengths`: lengths of the 128 packed documents in packing order; they sum to 8192, and the longest has exactly 2048 tokens.
All inputs are finite; a program needn't handle non-finite values.
Results may differ from a plain program's by a relative error of at most 0.017.
Values may be sent and summed in bfloat16 or wider, within the bound.
A program may use at most 192 MiB of HBM per device.

v0:
```python
import jax
import jax.numpy as jnp
from jax import lax
from jax.sharding import PartitionSpec as P

DK = 128
DV = 128
SPAN = 64


PRECISE = lax.Precision.HIGHEST


def passed_along(value, axis, by):
    devices = lax.axis_size(axis)
    pairs = [(i, i + by) for i in range(devices) if 0 <= i + by < devices]
    return lax.ppermute(value, axis, pairs)


def carried_in(value, axis, combine, identity):
    devices, mine = (lax.axis_size(axis), lax.axis_index(axis))
    everything = jax.tree.map(
        lambda part, kind: lax.all_gather(part.astype(kind), axis),
        value,
        (jnp.bfloat16, jnp.bfloat16),
    )
    start = jax.tree.map(
        lambda part, zero: jnp.broadcast_to(jnp.asarray(zero, part.dtype), part.shape),
        value,
        identity,
    )

    def hop(k, before):
        reached = k < mine
        new = combine(
            before, jax.tree.map(lambda part, own: part[k].astype(own.dtype), everything, value)
        )
        return jax.tree.map(lambda a, b: jnp.where(reached, a, b), new, before)

    return lax.fori_loop(0, devices, hop, start)


def shard_conv(before, current, weight, keep_masks):
    margin = weight.shape[0] - 1
    count_rows = current.shape[0]
    padded = jnp.concatenate([before, current], axis=0).astype(jnp.float32)
    summed = jnp.zeros((count_rows, current.shape[1]), jnp.float32)
    for offset in range(margin + 1):
        summed = (
            summed
            + weight[offset][None, :]
            * padded[offset : offset + count_rows]
            * keep_masks[margin - offset][:, None]
        )
    return jax.nn.silu(summed)


def unit_heads(vectors, head_count):
    reshaped = vectors.reshape(vectors.shape[0], head_count, -1)
    return reshaped / jnp.sqrt(jnp.sum(reshaped * reshaped, axis=-1, keepdims=True) + 1e-06)


def span_terms(queries, keys_unit, values, log_gamma, beta_values, resets):
    length = resets.shape[0]
    segment = jnp.cumsum(resets)
    cumulative = jnp.cumsum(log_gamma, axis=-1)
    row_index = jnp.arange(length, dtype=jnp.int32)[:, None]
    col_index = jnp.arange(length, dtype=jnp.int32)[None, :]
    same_doc = (segment[:, None] == segment[None, :]) & (row_index >= col_index)
    strict = same_doc & (row_index > col_index)
    log_ratio = cumulative[:, :, None] - cumulative[:, None, :]
    decay_pairs = jnp.exp(jnp.where(same_doc[None], log_ratio, -1e30))
    key_gram = jnp.einsum("hid,hjd->hij", keys_unit, keys_unit, precision=PRECISE)
    lower_part = jnp.where(strict[None], beta_values[:, :, None] * key_gram * decay_pairs, 0.0)
    head_start = jnp.where(segment[None, :] == 0, jnp.exp(cumulative), 0.0)
    last_segment = segment[length - 1]
    to_end = jnp.where(
        segment[None, :] == last_segment, jnp.exp(cumulative[:, length - 1 :] - cumulative), 0.0
    )
    through = jnp.where(last_segment == 0, jnp.exp(cumulative[:, length - 1]), 0.0)
    values_in = lax.linalg.triangular_solve(
        lower_part, beta_values[:, :, None] * values, left_side=True, lower=True, unit_diagonal=True
    )
    keys_in = lax.linalg.triangular_solve(
        lower_part,
        (beta_values * head_start)[:, :, None] * keys_unit,
        left_side=True,
        lower=True,
        unit_diagonal=True,
    )
    scores = jnp.einsum("hid,hjd->hij", queries, keys_unit, precision=PRECISE)
    inside = jnp.where(same_doc[None], scores * decay_pairs, 0.0)
    return (values_in, keys_in, inside, head_start, to_end, through)


def body(
    query_in,
    key_in,
    value_in,
    gate_in,
    conv_query,
    conv_key,
    conv_value,
    decay_in,
    beta_in,
    norm_gain,
    doc_lengths,
    out_weight,
):
    count_rows = query_in.shape[0]
    margin = conv_query.shape[0] - 1
    key_width = query_in.shape[1]
    value_heads = decay_in.shape[0]
    key_heads = key_width // DK
    tail_rows = jnp.concatenate(
        [
            query_in[count_rows - margin :],
            key_in[count_rows - margin :],
            value_in[count_rows - margin :],
        ],
        axis=1,
    )
    before = passed_along(tail_rows, "ctx", 1)
    first_row = lax.axis_index("ctx") * count_rows
    positions = first_row - margin + jnp.arange(count_rows + margin, dtype=jnp.int32)
    doc_starts = jnp.cumsum(doc_lengths) - doc_lengths
    start_flags = jnp.any(positions[:, None] == doc_starts[None, :], axis=1).astype(jnp.int32)
    running = jnp.cumsum(start_flags)
    keep_masks = [
        (
            running[margin:] - running[margin - lag_steps : margin - lag_steps + count_rows] == 0
        ).astype(jnp.float32)
        for lag_steps in range(margin + 1)
    ]
    resets = start_flags[margin:]
    queries = unit_heads(
        shard_conv(before[:, :key_width], query_in, conv_query, keep_masks), key_heads
    )
    keys_unit = unit_heads(
        shard_conv(before[:, key_width : 2 * key_width], key_in, conv_key, keep_masks), key_heads
    )
    values = shard_conv(before[:, 2 * key_width :], value_in, conv_value, keep_masks).reshape(
        count_rows, value_heads, DV
    )
    group_ratio = value_heads // key_heads
    queries = jnp.repeat(queries, group_ratio, axis=1)
    keys_unit = jnp.repeat(keys_unit, group_ratio, axis=1)
    log_gamma = -jax.nn.softplus(decay_in)
    beta_values = jax.nn.sigmoid(beta_in)
    spans = count_rows // SPAN

    def blocks(array):
        return array.reshape(spans, SPAN, value_heads, array.shape[-1]).transpose(0, 2, 1, 3)

    def gate_blocks(array):
        return array.reshape(value_heads, spans, SPAN).transpose(1, 0, 2)

    query_blocks = blocks(queries)
    key_blocks = blocks(keys_unit)
    value_blocks = blocks(values)
    values_in, keys_in, inside, head_start, to_end, through = jax.vmap(span_terms)(
        query_blocks,
        key_blocks,
        value_blocks,
        gate_blocks(log_gamma),
        gate_blocks(beta_values),
        resets.reshape(spans, SPAN),
    )
    key_end = key_blocks * to_end[..., None]
    zeros_state = jnp.zeros((value_heads, DK, DV), jnp.float32)
    identity = jnp.broadcast_to(jnp.eye(DK, dtype=jnp.float32), (value_heads, DK, DK))

    def state_step(carried, inputs):
        values_part, keys_part, end_keys, passing = inputs
        fresh_values = values_part - jnp.einsum(
            "hcd,hde->hce", keys_part, carried, precision=PRECISE
        )
        carried = passing[:, None, None] * carried + jnp.einsum(
            "hcd,hce->hde", end_keys, fresh_values, precision=PRECISE
        )
        return (carried, None)

    local_state, _ = lax.scan(state_step, zeros_state, (values_in, keys_in, key_end, through))

    def transition_step(carried, inputs):
        keys_part, end_keys, passing = inputs
        moved_rows = jnp.einsum("hcd,hde->hce", keys_part, carried, precision=PRECISE)
        return (
            passing[:, None, None] * carried
            - jnp.einsum("hcd,hce->hde", end_keys, moved_rows, precision=PRECISE),
            None,
        )

    final_map, _ = lax.scan(transition_step, identity, (keys_in, key_end, through))

    def compose(earlier, later):
        joined_map = jnp.einsum("hij,hjk->hik", later[0], earlier[0], precision=PRECISE)
        joined_state = (
            jnp.einsum("hij,hjk->hik", later[0], earlier[1], precision=PRECISE) + later[1]
        )
        return (joined_map, joined_state)

    prefix = carried_in((final_map, local_state), "ctx", compose, (identity, zeros_state))
    incoming = prefix[1]

    def output_step(carried, inputs):
        values_part, keys_part, query_part, inside_part, start_part, end_keys, passing = inputs
        fresh_values = values_part - jnp.einsum(
            "hcd,hde->hce", keys_part, carried, precision=PRECISE
        )
        result = jnp.einsum(
            "hcd,hde->hce", query_part * start_part[..., None], carried, precision=PRECISE
        ) + jnp.einsum("hij,hje->hie", inside_part, fresh_values, precision=PRECISE)
        carried = passing[:, None, None] * carried + jnp.einsum(
            "hcd,hce->hde", end_keys, fresh_values, precision=PRECISE
        )
        return (carried, result)

    _, results = lax.scan(
        output_step,
        incoming,
        (values_in, keys_in, query_blocks, inside, head_start, key_end, through),
    )
    heads_out = results.transpose(0, 2, 1, 3).reshape(count_rows, value_heads, DV)
    gate_values = gate_in.astype(jnp.float32).reshape(count_rows, value_heads, DV)
    normed = (
        heads_out
        / jnp.sqrt(jnp.mean(heads_out * heads_out, axis=-1, keepdims=True) + 1e-06)
        * norm_gain
        * jax.nn.silu(gate_values)
    )
    mixed_rows = normed.reshape(count_rows, value_heads * DV).astype(jnp.bfloat16)
    return lax.psum_scatter(
        lax.dot_general(
            out_weight, mixed_rows, (((0,), (1,)), ((), ())), preferred_element_type=jnp.float32
        ).astype(jnp.bfloat16),
        "head",
        scatter_dimension=0,
        tiled=True,
    )


def solution(mesh):
    return jax.shard_map(
        body,
        mesh=mesh,
        in_specs=(
            P("ctx", "head"),
            P("ctx", "head"),
            P("ctx", "head"),
            P("ctx", "head"),
            P(None, "head"),
            P(None, "head"),
            P(None, "head"),
            P("head", "ctx"),
            P("head", "ctx"),
            P(),
            P(),
            P("head", None),
        ),
        out_specs=P("head", "ctx"),
        check_vma=False,
    )
```

profile of v0, /device:TPU:24, one launch (start us, length us, event | category | flops | bytes accessed | tf_op | source)
XLA Modules:
  0.0 457.9 jit_solution(8664755651306898443)
XLA Ops:
  8.7 1.9 collective-permute-start
  22.3 78.6 %custom-call.6 = f32[2,8,1,64,64]{3,4,2,1,0:T(8,128)S(1)} custom-call(f32[2,8,1,64,64]{4,3,2,1,0:T(8,128)S(1)} %fusion.49), custom_call_target="InvertDiagBlocksLowerTriangular" | custom-call | tf_op jit(solution)/shard_map/vmap()/triangular_solve/custom-call.1 | solution.py:84
  105.1 3.5 while.49
  109.5 3.5 while.47
  114.8 2.0 fusion.44
  116.8 94.2 %all-gather.7.cloned.1.call-done = bf16[512,128,128]{2,1,0:T(8,128)(2,1)} async-done(((bf16[8,128,128]{2,1,0:T(8,128)(2,1)}), bf16[512,128,128]{2,1,0:T(8,128)(2,1)}) %all-gather.7.cloned.1.call-update) | async-done | bytes 16777232 | tf_op jit(solution)/shard_map/all_gather | solution.py:23
  211.0 99.7 %all-gather.5.cloned.1.call-done = bf16[512,128,128]{2,1,0:T(8,128)(2,1)} async-done(((bf16[8,128,128]{2,1,0:T(8,128)(2,1)}), bf16[512,128,128]{2,1,0:T(8,128)(2,1)}) %all-gather.5.cloned.1.call-update) | async-done | bytes 16777232 | tf_op jit(solution)/shard_map/all_gather | solution.py:23
  310.7 102.1 %while.50 = (s32[]{:T(128)}, f32[8,128,128]{2,1,0:T(8,128)S(1)}, s32[]{:T(128)}, bf16[64,8,128,128]{3,2,1,0:T(8,128)(2,1)}, bf16[64,8,128,128]{3,2,1,0:T(8,128)(2,1)}, /*index=5*/s32[]{:T(128)}, s32[]{:T(128)}) while((s32[]{:T(128)}, f32[8,128,128]{2,1,0:T(8,128)S(1)}, s32[]{:T(128)}, bf16[64,8,128,128]{3,2,1,0:T(8,128)(2,1)}, ...), condition=%wide.region_12.14_spmd.clone, body=%wide.region_11.13_spmd.clone.sunk | while | flops 201981952 | bytes 3148383 | solution.py:40
  318.8 1.5 fusion.152
  320.3 1.5 fusion.152
  321.9 1.5 fusion.152
  326.7 1.5 fusion.152
  328.3 1.5 fusion.152
  329.9 1.5 fusion.152
  334.7 1.5 fusion.152
  336.3 1.5 fusion.152
  337.9 1.5 fusion.152
  342.7 1.5 fusion.152
  344.3 1.5 fusion.152
  345.9 1.5 fusion.152
  412.8 7.0 %while.48 = (s32[]{:T(128)}, f32[8,128,128]{2,1,0:T(8,128)S(1)}, f32[2,8,64,128]{3,2,1,0:T(8,128)}, f32[2,8]{1,0:T(2,128)S(1)}, f32[2,8,64,128]{3,2,1,0:T(8,128)...) while((s32[]{:T(128)}, f32[8,128,128]{2,1,0:T(8,128)S(1)}, ...), condition=%wide.region_15.17_spmd, body=%wide.region_14.16_spmd.sunk | while | flops 352780288 | bytes 4991677 | solution.py:219
  422.7 3.9 fusion.43
  426.7 23.0 %reduce-scatter.2.cloned.1.call-done = bf16[512,128]{0,1:T(8,128)(2,1)} async-done(((bf16[2048,128]{0,1:T(8,128)(2,1)}), bf16[512,128]{0,1:T(8,128)(2,1)}) %reduce-scatter.2.cloned.1.call-update) | async-done | bytes 131088 | tf_op jit(solution)/shard_map/reduce_scatter | solution.py:233
  449.7 1.7 copy.111
  (233 shorter events, 118.4 us)
Async XLA Ops:
  6.5 107.6 %copy-start = (f32[128]{0:T(128)S(1)}, f32[128]{0:T(128)}, u32[]{:S(2)}) copy-start(f32[128]{0:T(128)} %param.31) | copy-start | bytes 1540
  6.5 204.5 %all-gather.7.cloned.1.call-start = ((), (), s32[]{:S(2)}) async-start(), calls=%async_computation.3 | async-start | bytes 17039360 | tf_op jit(solution)/shard_map/all_gather | solution.py:23
  8.7 10.5 %collective-permute-start = (bf16[3,2048]{1,0:T(4,128)(2,1)S(1)}, bf16[3,2048]{1,0:T(4,128)(2,1)S(1)}, u32[]{:S(2)}, u32[]{:S(2)}) collective-permute-start(bf16[3,2048]{1,0:T(4,128)(2,1)S(1)} %pad_maximum_fusion), channel_id=1, source_target_pairs={{0,4},{4,8},{8,12},{12,16},{16,20},{20,24},{24,28},{28,32},{32,36}... | collective-permute-start | bytes 36872 | tf_op jit(solution)/shard_map/ppermute | solution.py:17
  21.3 82.8 %copy-start.1 = (f32[128,4,2,128]{3,0,2,1:T(8,128)}, f32[128,4,2,128]{3,0,2,1:T(8,128)S(1)}, u32[]{:S(2)}) copy-start(f32[128,4,2,128]{3,0,2,1:T(8,128)S(1)} %broadcast_in_dim.112) | copy-start | bytes 1572868
  109.4 201.3 %all-gather.5.cloned.1.call-start = ((), (), s32[]{:S(2)}) async-start(), calls=%async_computation.2 | async-start | bytes 17039360 | tf_op jit(solution)/shard_map/all_gather | solution.py:23
  113.9 335.8 %reduce-scatter.2.cloned.1.call-start = ((), (), s32[]{:S(2)}) async-start(), calls=%async_computation.1 | async-start | bytes 655360 | tf_op jit(solution)/shard_map/reduce_scatter | solution.py:233
Sparse Core Ops, SparseCore 0:
  109.5 101.4 all-gather.6
  213.8 96.8 all-gather.4
  426.8 22.8 reduce-scatter.1
where the time goes:
time: 460 us; the launch traced here: 458 us
  waiting for transfers between devices  217 us (47%)
  matrix products  120 us (26%)
  other arithmetic  89.8 us (20%)
  between operations  13.5 us (3%)
  local copies, waits for them, and re-layouts  12.6 us (3%)
    all_gather x2, waiting for transfers between devices, carried_in(): lax.all_gather(part.astype(kind), axis)  194 us
    dot_general x64, matrix products, compose(): jnp.einsum('hij,hjk->hik', later[0], earlier[1], precision=PRECISE)  97.4 us
    another operation x3, other arithmetic, span_terms(): lax.linalg.triangular_solve(lower_part, (beta_values * head_start)[:, :,...  78.7 us
    reduce_scatter x1, waiting for transfers between devices, body(): lax.psum_scatter(lax.dot_general(out_weight, mixed_rows, (((0,), (1,)), (...  23 us
  transfers between devices with their start and end apart: 4, of which 3 were waited for; matrix products, arithmetic and copies ran while one was open for 3% of the time, Pallas kernels for 0%

commit v1 on v0

v1 whole, which is shorter than its diff:
```python
import jax
import jax.numpy as jnp
from jax import lax
from jax.experimental import pallas as pl
from jax.experimental.pallas import tpu as pltpu
from jax.sharding import PartitionSpec as P

MESH = pl.DeviceIdType.MESH
F32, BF16 = jnp.float32, jnp.bfloat16
DK = 128
ROWS = 128
TOK = 256
HALO = 16
CHIPS = 8
OWN = 4


def dot(a, b):
    return jnp.dot(a, b, preferred_element_type=F32)


def kernel(
    q_hbm, k_hbm, v_hbm, g_hbm, dec_hbm, beta_hbm, w_hbm,
    cq_ref, ck_ref, cv_ref, docs_ref, gain_ref,
    out_ref,
    qx, kx, vx, gx, dx, bx, xf, w_vm,
    mb, qeff, oloc, rbuf, q8, s0buf, sout, sbuf, mx, mixfull, sendp, recvp,
    lsem, xs, xr, hs, hr, as_, ar, ys, yr, ss, sr, ms, mr, ps, pr,
):
    ctx, x = lax.axis_index("ctx"), lax.axis_index("head")
    n_ctx, n_x = lax.axis_size("ctx"), lax.axis_size("head")
    c = lax.rem(ctx, 2)
    chip = ctx // 2
    z = lax.rem(chip, CHIPS)
    line = ctx - 2 * z - c
    n_chips = n_ctx // 2
    partner = chip * 2 + 1 - c
    prev_tail = lax.rem(chip + n_chips - 1, n_chips) * 2 + 1
    next_head = lax.rem(chip + 1, n_chips) * 2
    own = z // OWN == c
    head_at = z - OWN * c
    up = lax.rem(ctx + 2 * CHIPS, n_ctx)
    down = lax.rem(ctx + n_ctx - 2 * CHIPS, n_ctx)

    def at(chip_z):
        return line + 2 * chip_z + c

    w_copy = pltpu.make_async_copy(w_hbm, w_vm, lsem.at[0])
    w_copy.start()
    cols = lambda core, width: pl.ds(pl.multiple_of(core * width, 128), width)
    mine = pl.ds(pl.multiple_of(HALO + ROWS * c, 16), ROWS)
    gmine = pl.ds(pl.multiple_of(ROWS * c, 16), ROWS)
    local = []
    for n, (src, dst) in enumerate((
        (q_hbm.at[:, cols(c, 256)], qx.at[mine]),
        (k_hbm.at[:, cols(c, 256)], kx.at[mine]),
        (v_hbm.at[:, cols(c, 512)], vx.at[mine]),
        (g_hbm.at[:, cols(c, 512)], gx.at[gmine]),
        (dec_hbm, dx.at[c]),
        (beta_hbm, bx.at[c]),
    )):
        local.append(pltpu.make_async_copy(src, dst, lsem.at[n + 1]))
        local[-1].start()

    barrier = pltpu.get_barrier_semaphore()

    def greet(**device):
        pl.semaphore_signal(barrier, inc=1, device_id=device, device_id_type=MESH)

    greet(ctx=partner)
    greet(ctx=prev_tail)
    for k in range(1, 4):
        greet(head=lax.rem(x + k, n_x))
    for i in range(OWN):
        owner = OWN * c + i

        @pl.when(z != owner)
        def _():
            greet(ctx=at(owner))

    @pl.when(own)
    def _():
        greet(ctx=down)
        for k in range(1, CHIPS):
            greet(ctx=at(lax.rem(z + k, CHIPS)))

    expect = 1 + 2 * c + 3 + jnp.where(own, OWN - 1 + CHIPS - 1 + 1, OWN)
    pl.semaphore_wait(barrier, expect)

    tail = pl.ds(ROWS - HALO, HALO)
    front = pl.ds(0, HALO)
    halo = []
    for core in range(2):
        for n, (src, dst, width) in enumerate(((q_hbm, qx, 256), (k_hbm, kx, 256), (v_hbm, vx, 512))):
            halo.append(pltpu.make_async_remote_copy(
                src.at[tail, pl.ds(core * width, width)], dst.at[front],
                hs.at[core, n], hr.at[n], device_id={"ctx": next_head + core}, device_id_type=MESH,
            ))

    @pl.when(c == 1)
    def _():
        for copy in halo:
            copy.start()

    trade = []
    for n, (src, dst) in enumerate((
        (dec_hbm, dx.at[c]),
        (beta_hbm, bx.at[c]),
        (k_hbm.at[:, cols(1 - c, 256)], kx.at[mine]),
        (q_hbm.at[:, cols(1 - c, 256)], qx.at[mine]),
        (v_hbm.at[:, cols(1 - c, 512)], vx.at[mine]),
        (g_hbm.at[:, cols(1 - c, 512)], gx.at[gmine]),
    )):
        trade.append(pltpu.make_async_remote_copy(
            src, dst, xs.at[n], xr.at[n], device_id={"ctx": partner}, device_id_type=MESH,
        ))
        trade[-1].start()

    first = chip * TOK
    sub = lax.broadcasted_iota(jnp.int32, (128, 128), 0)
    lane = lax.broadcasted_iota(jnp.int32, (128, 128), 1)
    lens = jnp.broadcast_to(docs_ref[...].astype(F32), (128, 128))
    starts_col = jnp.sum(jnp.where(lane < sub, lens, 0.0), axis=1, keepdims=True)
    starts_row = jnp.sum(jnp.where(sub < lane, lens.T, 0.0), axis=0, keepdims=True)
    pos_row = (first + lax.broadcasted_iota(jnp.int32, (128, TOK), 1)).astype(F32)
    seg_row = jnp.sum(jnp.where(starts_col <= pos_row, 1.0, 0.0), axis=0, keepdims=True)
    seg_prev = jnp.sum(jnp.where(starts_col <= (first - 1).astype(F32), 1.0, 0.0), axis=0, keepdims=True)
    seg_end = jnp.sum(jnp.where(starts_col <= (first + TOK - 1).astype(F32), 1.0, 0.0), axis=0, keepdims=True)
    pos_col = first + lax.broadcasted_iota(jnp.int32, (TOK, 128), 0)

    def seg_at(back):
        return jnp.sum(jnp.where(starts_row <= (pos_col - back).astype(F32), 1.0, 0.0), axis=1, keepdims=True)

    seg_col = seg_at(0)
    keeps = [None] + [(seg_at(j) == seg_col).astype(F32) for j in range(1, 4)]
    row_i = lax.broadcasted_iota(jnp.int32, (TOK, TOK), 0)
    col_i = lax.broadcasted_iota(jnp.int32, (TOK, TOK), 1)
    same_doc = (seg_col == seg_row) & (row_i >= col_i)
    eye = (row_i == col_i).astype(F32)
    upper = (row_i <= col_i).astype(F32)

    for copy in local:
        copy.wait()
    for copy in trade:
        copy.wait_recv()

    decay = jnp.concatenate([dx[0], dx[1]], axis=1)
    log_gamma = -jax.nn.softplus(decay)
    cum8 = jnp.dot(log_gamma, upper, precision=lax.Precision.HIGHEST, preferred_element_type=F32)
    beta8 = jax.nn.sigmoid(jnp.concatenate([bx[0], bx[1]], axis=1))
    pick = lambda rows: jnp.where(c == 0, rows[:OWN], rows[OWN:])
    cum, beta = pick(cum8), pick(beta8)
    last = cum[:, TOK - 1:]
    to_end = jnp.where(seg_row == seg_end, jnp.exp(last - cum), 0.0)
    through = jnp.where(seg_end == seg_prev, jnp.exp(last), 0.0)
    by_token = jnp.concatenate([cum, beta], axis=0).T
    in_first = seg_col == seg_prev

    for n in range(3):
        halo[n].wait_recv()

    for ref, lo, width in ((qx, 0, 256), (kx, 256, 256), (vx, 512, 512)):
        xf[:, lo:lo + width] = ref[...].astype(F32)

    def conv(w_ref, lo, width):
        taps = w_ref[:, cols(c, width)]
        total = None
        for i in range(4):
            term = taps[i:i + 1] * xf[HALO - 3 + i:HALO - 3 + i + TOK, lo:lo + width]
            if i < 3:
                term = term * keeps[3 - i]
            total = term if total is None else total + term
        return total * jax.nn.sigmoid(total)

    def unit(rows):
        return rows * lax.rsqrt(jnp.sum(rows * rows, axis=-1, keepdims=True) + 1e-6)

    q_all, k_all = conv(cq_ref, 0, 256), conv(ck_ref, 256, 256)
    v_all = conv(cv_ref, 512, 512)

    block = lambda size: (row_i // size) == (col_i // size)
    cuts = [block(16)]
    for size in (16, 32, 64, 128):
        cuts.append(block(2 * size) & ~block(size) if size < 128 else ~block(size))

    sends = []
    for kh in range(2):
        kf = unit(k_all[:, kh * DK:(kh + 1) * DK])
        qf = unit(q_all[:, kh * DK:(kh + 1) * DK])
        kb, qb = kf.astype(BF16), qf.astype(BF16)
        k_t = kf.T
        k_tb = k_t.astype(BF16)
        gram = dot(kb, k_tb)
        scores = dot(qb, k_tb)
        for i in (2 * kh, 2 * kh + 1):
            cum_col = by_token[:, i:i + 1]
            beta_col = by_token[:, OWN + i:OWN + i + 1]
            start_col = jnp.where(in_first, jnp.exp(cum_col), 0.0)
            pairs = jnp.exp(jnp.where(same_doc, cum_col - cum[i:i + 1], -1e30))
            low = jnp.where(row_i > col_i, beta_col * gram * pairs, 0.0)
            inside = (scores * pairs).astype(BF16)
            n1f = jnp.where(cuts[0], -low, 0.0)
            n1 = n1f.astype(BF16)
            n2 = dot(n1, n1).astype(BF16)
            n4 = dot(n2, n2).astype(BF16)
            n8 = dot(n4, n4).astype(BF16)
            t = eye + n1f
            for power in (n2, n4, n8):
                t = t + dot(t.astype(BF16), power)
            for cut in cuts[1:]:
                edge = jnp.where(cut, low, 0.0).astype(BF16)
                tb = t.astype(BF16)
                t = t - dot(tb, dot(edge, tb).astype(BF16))
            v = v_all[:, i * DK:(i + 1) * DK]
            rhs = jnp.concatenate([beta_col * v, (beta_col * start_col) * kf], axis=1).astype(BF16)
            uw = dot(t.astype(BF16), rhs).astype(BF16)
            k_end = (k_t * to_end[i:i + 1]).astype(BF16)
            kuw = dot(k_end, uw)
            iuw = dot(inside, uw)
            mb[i, :, :DK] = (through[i:i + 1] * eye[:DK, :DK] - kuw[:, DK:]).astype(BF16)
            mb[i, :, DK:] = kuw[:, :DK].astype(BF16)
            owner = OWN * c + i
            send = pltpu.make_async_remote_copy(
                mb.at[i], rbuf.at[z], as_.at[i], ar.at[z], device_id={"ctx": at(owner)}, device_id_type=MESH,
            )
            sends.append((owner, send))

            @pl.when(z != owner)
            def _():
                send.start()

            @pl.when(z == owner)
            def _():
                rbuf[z] = mb[i]

            oloc[i] = iuw[:, :DK]
            qeff[i] = (qf * start_col - iuw[:, DK:]).astype(BF16)

    back = []
    for j in range(CHIPS):
        back.append(pltpu.make_async_remote_copy(
            sout.at[j], sbuf.at[jnp.where(own, head_at, 0)], ss.at[j], sr.at[jnp.where(own, head_at, 0)],
            device_id={"ctx": at(j)}, device_id_type=MESH,
        ))
    ahead = pltpu.make_async_remote_copy(q8, s0buf, ys, yr, device_id={"ctx": up}, device_id_type=MESH)

    @pl.when(own)
    def _():
        for j in range(CHIPS):
            @pl.when(z != j)
            def _():
                pltpu.make_async_remote_copy(
                    mb.at[0], rbuf.at[j], as_.at[0], ar.at[j], device_id={"ctx": at(j)}, device_id_type=MESH,
                ).wait_recv()

        def then(later, earlier):
            joined = dot(later[:, :DK], earlier)
            return jnp.concatenate([joined[:, :DK], joined[:, DK:] + later[:, DK:].astype(F32)], axis=1).astype(BF16)

        one = [rbuf[j] for j in range(CHIPS)]
        two = [then(one[2 * j + 1], one[2 * j]) for j in range(4)]
        four = [then(two[1], two[0]), then(two[3], two[2])]
        q8[...] = (dot(four[1][:, :DK], four[0][:, DK:]) + four[1][:, DK:].astype(F32)).astype(BF16)
        ahead.start()
        six = then(two[2], four[0])
        pre = [None, one[0], two[0], then(one[2], two[0]), four[0], then(one[4], four[0]), six, then(one[6], six)]
        ahead.wait_recv()
        s0 = jnp.where(ctx >= 2 * CHIPS, s0buf[...].astype(F32), 0.0).astype(BF16)
        for j in (4, 3, 5, 2, 6, 1, 7, 0):
            if j == 0:
                state = s0
            else:
                state = (dot(pre[j][:, :DK], s0) + pre[j][:, DK:].astype(F32)).astype(BF16)
            sout[j] = state

            @pl.when(z != j)
            def _():
                back[j].start()

            @pl.when(z == j)
            def _():
                sbuf[head_at] = state

    swaps = []
    for i in range(OWN):
        @pl.when(z != OWN * c + i)
        def _():
            pltpu.make_async_remote_copy(
                sout.at[0], sbuf.at[i], ss.at[0], sr.at[i], device_id={"ctx": partner}, device_id_type=MESH,
            ).wait_recv()

        o = oloc[i] + dot(qeff[i], sbuf[i])
        gate = gx[:, i * DK:(i + 1) * DK].astype(F32)
        normed = o * lax.rsqrt(jnp.mean(o * o, axis=-1, keepdims=True) + 1e-6)
        mx[:, i * DK:(i + 1) * DK] = (normed * gain_ref[...] * (gate * jax.nn.sigmoid(gate))).astype(BF16)
        here = cols(OWN * c + i, DK)
        swaps.append(pltpu.make_async_remote_copy(
            mx.at[pl.ds(pl.multiple_of(ROWS * (1 - c), 16), ROWS), pl.ds(i * DK, DK)], mixfull.at[:, here],
            ms.at[i], mr.at[i], device_id={"ctx": partner}, device_id_type=MESH,
        ))
        swaps[-1].start()
        mixfull[:, here] = mx[gmine, i * DK:(i + 1) * DK]
    for swap in swaps:
        swap.wait_recv()
    w_copy.wait()

    mixed = mixfull[...]
    width = w_vm.shape[1] // 4
    parts = []
    for k in (2, 1, 3):
        to = lax.rem(x + k, n_x)
        sendp[k - 1] = dot(mixed, w_vm[:, cols(to, width)]).astype(BF16)
        parts.append(pltpu.make_async_remote_copy(
            sendp.at[k - 1], recvp.at[k - 1], ps.at[k - 1], pr.at[k - 1], device_id={"head": to}, device_id_type=MESH,
        ))
        parts[-1].start()
    total = dot(mixed, w_vm[:, cols(x, width)]).astype(BF16).astype(F32)
    for part, k in zip(parts, (2, 1, 3)):
        part.wait_recv()
        total = total + recvp[k - 1].astype(F32)
    out_ref[...] = total.T.astype(BF16)

    for copy in trade + swaps + parts:
        copy.wait_send()

    @pl.when(c == 1)
    def _():
        for copy in halo:
            copy.wait_send()

    for owner, send in sends:
        @pl.when(z != owner)
        def _():
            send.wait_send()

    @pl.when(own)
    def _():
        ahead.wait_send()
        for j in range(CHIPS):
            @pl.when(z != j)
            def _():
                back[j].wait_send()


def body(
    query_in, key_in, value_in, gate_in, conv_query, conv_key, conv_value,
    decay_in, beta_in, norm_gain, doc_lengths, out_weight,
):
    anywhere, vmem = pl.BlockSpec(memory_space=pl.ANY), pl.BlockSpec(memory_space=pltpu.VMEM)
    dma = pltpu.SemaphoreType.DMA
    features = out_weight.shape[1] // 4
    return pl.pallas_call(
        kernel,
        out_shape=jax.ShapeDtypeStruct((features, ROWS), BF16),
        in_specs=[anywhere] * 7 + [vmem] * 5,
        out_specs=vmem,
        scratch_shapes=[
            pltpu.VMEM((HALO + TOK, 256), BF16),
            pltpu.VMEM((HALO + TOK, 256), BF16),
            pltpu.VMEM((HALO + TOK, 512), BF16),
            pltpu.VMEM((TOK, 512), BF16),
            pltpu.VMEM((2, 8, ROWS), F32),
            pltpu.VMEM((2, 8, ROWS), F32),
            pltpu.VMEM((HALO + TOK, 1024), F32),
            pltpu.VMEM(out_weight.shape, BF16),
            pltpu.VMEM((OWN, DK, 2 * DK), BF16),
            pltpu.VMEM((OWN, TOK, DK), BF16),
            pltpu.VMEM((OWN, TOK, DK), F32),
            pltpu.VMEM((CHIPS, DK, 2 * DK), BF16),
            pltpu.VMEM((DK, DK), BF16),
            pltpu.VMEM((DK, DK), BF16),
            pltpu.VMEM((CHIPS, DK, DK), BF16),
            pltpu.VMEM((OWN, DK, DK), BF16),
            pltpu.VMEM((TOK, OWN * DK), BF16),
            pltpu.VMEM((ROWS, 2 * OWN * DK), BF16),
            pltpu.VMEM((3, ROWS, features), BF16),
            pltpu.VMEM((3, ROWS, features), BF16),
            dma((7,)), dma((6,)), dma((6,)), dma((2, 3)), dma((3,)),
            dma((OWN,)), dma((CHIPS,)), dma, dma, dma((CHIPS,)), dma((OWN,)),
            dma((OWN,)), dma((OWN,)), dma((3,)), dma((3,)),
        ],
        compiler_params=pltpu.CompilerParams(
            collective_id=0, has_side_effects=True, vmem_limit_bytes=56 << 20
        ),
        name="mixer",
    )(
        query_in, key_in, value_in, gate_in, decay_in, beta_in, out_weight,
        conv_query, conv_key, conv_value, doc_lengths.reshape(1, -1), norm_gain.reshape(1, -1),
    )


def solution(mesh):
    return jax.shard_map(
        body,
        mesh=mesh,
        in_specs=(
            P("ctx", "head"), P("ctx", "head"), P("ctx", "head"), P("ctx", "head"),
            P(None, "head"), P(None, "head"), P(None, "head"),
            P("head", "ctx"), P("head", "ctx"), P(), P(), P("head", None),
        ),
        out_specs=P("head", "ctx"),
        check_vma=False,
    )
```

time: 460 us -> 54.5 us (0.12)
  the two profiles are of different devices: /device:TPU:24 before, /device:TPU:1 now
where the time goes in v1:
time: 54.5 us; the launch traced here: 54.3 us
  Pallas kernels  52.7 us (97%)
  local copies, waits for them, and re-layouts  1.57 us (3%)
    pallas_call x1, Pallas kernels, body(): pl.pallas_call(kernel, out_shape=jax.ShapeDtypeStruct((features, ROWS), B...  52.7 us
    unnamed x1, local copies, waits for them, and re-layouts  1.57 us

profile of v1, /device:TPU:1, one launch (start us, length us, event | category | flops | bytes accessed | tf_op | source)
XLA Modules:
  0.0 54.3 jit_solution(15384579639568352626)
XLA Ops:
  0.0 52.7 %mixer.1 = bf16[512,128]{1,0:T(8,128)(2,1)} custom-call(bf16[128,512]{1,0:T(8,128)(2,1)} %q_hbm.1, bf16[128,512]{1,0:T(8,128)(2,1)} %k_hbm.1, bf16[128,1024]{1,0:T(8,128)(2,1)} %v_hbm.1, bf16[128,1024]{1,0:T(8,128)(2,1)} %g_hbm.1, f32[8,128]{1,0:T(8,128)} %dec_hbm.1, f32[8,128]{1,0:T(8,128)} %beta_hbm.1, bf16[1024,2048]{1,0:T(8,128)(2,1)} %w_hbm.1, ...), custom_call_target="tpu_custom_call" | custom-call | tf_op jit(solution)/shard_map/mixer/pallas_call | solution.py:352
  52.7 1.6 %copy.14 = bf16[512,128]{1,0:T(8,128)(2,1)} copy(bf16[512,128]{1,0:T(8,128)(2,1)} %mixer.1) | data formatting | bytes 262144

commit v2 on v1

v2 whole, which is shorter than its diff:
```python
import jax
import jax.numpy as jnp
from jax import lax
from jax.experimental import pallas as pl
from jax.experimental.pallas import tpu as pltpu
from jax.sharding import PartitionSpec as P

MESH = pl.DeviceIdType.MESH
F32, BF16 = jnp.float32, jnp.bfloat16
DK = 128
ROWS = 128
TOK = 256
HALO = 16
CHIPS = 8
OWN = 4


def dot(a, b):
    return jnp.dot(a, b, preferred_element_type=F32)


def kernel(
    q_hbm, k_hbm, v_hbm, g_hbm, dec_hbm, beta_hbm, w_hbm,
    cq_ref, ck_ref, cv_ref, docs_ref, gain_ref,
    out_ref,
    qx, kx, vx, gx, dx, bx, hb, hx, xf, act, w_vm,
    mb, qeff, oloc, rbuf, pre, q8, s0buf, sout, sbuf, gated, mx, mixfull, own_part, sendp, recvp,
    lsem, xs, xr, hl, hs, hr, as_, ar, ys, yr, ss, sr, ms, mr, ps, pr, told,
):
    ctx, x = lax.axis_index("ctx"), lax.axis_index("head")
    n_ctx, n_x = lax.axis_size("ctx"), lax.axis_size("head")
    c = lax.rem(ctx, 2)
    chip = ctx // 2
    z = lax.rem(chip, CHIPS)
    line = ctx - 2 * z - c
    n_chips = n_ctx // 2
    partner = chip * 2 + 1 - c
    prev_tail = jnp.maximum(chip - 1, 0) * 2 + 1
    next_head = jnp.minimum(chip + 1, n_chips - 1) * 2
    has_prev, has_next = chip > 0, chip < n_chips - 1
    sends_halo = (c == 1) & has_next
    own = z // OWN == c
    head_at = z - OWN * c
    has_up, has_down = ctx < n_ctx - 2 * CHIPS, ctx >= 2 * CHIPS
    up = jnp.minimum(ctx + 2 * CHIPS, n_ctx - 1)
    down = jnp.maximum(ctx - 2 * CHIPS, 0)

    def at(chip_z):
        return line + 2 * chip_z + c

    w_copy = pltpu.make_async_copy(w_hbm, w_vm, lsem.at[0])
    w_copy.start()
    cols = lambda core, width: pl.ds(pl.multiple_of(core * width, 128), width)
    mine = pl.ds(pl.multiple_of(ROWS * c, 16), ROWS)
    local = []
    for n, (src, dst) in enumerate((
        (q_hbm.at[:, cols(c, 256)], qx.at[mine]),
        (k_hbm.at[:, cols(c, 256)], kx.at[mine]),
        (v_hbm.at[:, cols(c, 512)], vx.at[mine]),
        (g_hbm.at[:, cols(c, 512)], gx.at[mine]),
        (dec_hbm, dx.at[c]),
        (beta_hbm, bx.at[c]),
    )):
        local.append(pltpu.make_async_copy(src, dst, lsem.at[n + 1]))
        local[-1].start()

    pack = []
    for core in range(2):
        for n, (src, lo, width) in enumerate(((q_hbm, 0, 256), (k_hbm, 256, 256), (v_hbm, 512, 512))):
            pack.append(pltpu.make_async_copy(
                src.at[pl.ds(ROWS - HALO, HALO), pl.ds(core * width, width)],
                hb.at[core, :, pl.ds(lo, width)], hl.at[core, n],
            ))

    @pl.when(sends_halo)
    def _():
        for copy in pack:
            copy.start()

    @pl.when(chip == 0)
    def _():
        hx[...] = jnp.zeros_like(hx)

    @pl.when(~has_down)
    def _():
        s0buf[...] = jnp.zeros_like(s0buf)

    barrier = pltpu.get_barrier_semaphore()

    def signal(sem, **device):
        pl.semaphore_signal(sem, inc=1, device_id=device, device_id_type=MESH)

    def ring(k):
        return at(lax.rem(z + k + CHIPS, CHIPS))

    x_next, x_prev = lax.rem(x + 1, n_x), lax.rem(x + n_x - 1, n_x)
    signal(barrier, ctx=partner)
    signal(barrier, head=x_next)
    signal(barrier, head=x_prev)
    signal(barrier, ctx=ring(1))
    signal(barrier, ctx=ring(-1))

    @pl.when(has_prev)
    def _():
        signal(barrier, ctx=prev_tail)

    @pl.when(has_down)
    def _():
        signal(barrier, ctx=down)

    pl.semaphore_wait(barrier, 5 + jnp.where(sends_halo, 2, 0) + jnp.where(has_up, 1, 0))

    halo = []
    for core in range(2):
        halo.append(pltpu.make_async_remote_copy(
            hb.at[core], hx, hs.at[core], hr, device_id={"ctx": next_head + core}, device_id_type=MESH,
        ))

    @pl.when(sends_halo)
    def _():
        for copy in pack:
            copy.wait()
        for copy in halo:
            copy.start()

    trade = []
    for n, (src, dst) in enumerate((
        (dec_hbm, dx.at[c]),
        (beta_hbm, bx.at[c]),
        (k_hbm.at[:, cols(1 - c, 256)], kx.at[mine]),
        (q_hbm.at[:, cols(1 - c, 256)], qx.at[mine]),
        (v_hbm.at[:, cols(1 - c, 512)], vx.at[mine]),
        (g_hbm.at[:, cols(1 - c, 512)], gx.at[mine]),
    )):
        trade.append(pltpu.make_async_remote_copy(
            src, dst, xs.at[n], xr.at[n], device_id={"ctx": partner}, device_id_type=MESH,
        ))
        trade[-1].start()

    signal(told.at[0], ctx=ring(1))
    signal(told.at[1], ctx=ring(-1))
    signal(told.at[2], head=x_next)

    first = chip * TOK
    sub = lax.broadcasted_iota(jnp.int32, (128, 128), 0)
    lane = lax.broadcasted_iota(jnp.int32, (128, 128), 1)
    lens = jnp.broadcast_to(docs_ref[...].astype(F32), (128, 128))
    starts_col = jnp.sum(jnp.where(lane < sub, lens, 0.0), axis=1, keepdims=True)
    starts_row = jnp.sum(jnp.where(sub < lane, lens.T, 0.0), axis=0, keepdims=True)
    pos_row = (first + lax.broadcasted_iota(jnp.int32, (128, TOK), 1)).astype(F32)
    seg_row = jnp.sum(jnp.where(starts_col <= pos_row, 1.0, 0.0), axis=0, keepdims=True)
    seg_prev = jnp.sum(jnp.where(starts_col <= (first - 1).astype(F32), 1.0, 0.0), axis=0, keepdims=True)
    seg_end = jnp.sum(jnp.where(starts_col <= (first + TOK - 1).astype(F32), 1.0, 0.0), axis=0, keepdims=True)
    pos_col = first + lax.broadcasted_iota(jnp.int32, (TOK, 128), 0)

    def seg_at(back):
        return jnp.sum(jnp.where(starts_row <= (pos_col - back).astype(F32), 1.0, 0.0), axis=1, keepdims=True)

    seg_col = seg_at(0)
    keeps = [None] + [(seg_at(j) == seg_col).astype(F32) for j in range(1, 4)]
    upper = (lax.broadcasted_iota(jnp.int32, (TOK, TOK), 0) <= lax.broadcasted_iota(jnp.int32, (TOK, TOK), 1)).astype(F32)
    halves = (slice(0, 128), slice(128, 256))
    quads = ((0, 0), (1, 0), (1, 1))
    same_doc = {}
    for r, s in quads:
        same = seg_col[halves[r]] == seg_row[:, halves[s]]
        same_doc[r, s] = same & (sub >= lane) if r == s else same

    for copy in local:
        copy.wait()
    for copy in trade[:5]:
        copy.wait_recv()

    pl.semaphore_wait(told.at[0], 1)
    pl.semaphore_wait(told.at[1], 1)
    signal(told.at[3], ctx=ring(2))
    signal(told.at[4], ctx=ring(-2))

    decay = jnp.concatenate([dx[0], dx[1]], axis=1)
    log_gamma = -jax.nn.softplus(decay)
    cum8 = jnp.dot(log_gamma, upper, precision=lax.Precision.HIGHEST, preferred_element_type=F32)
    beta8 = jax.nn.sigmoid(jnp.concatenate([bx[0], bx[1]], axis=1))
    pick = lambda rows: jnp.where(c == 0, rows[:OWN], rows[OWN:])
    cum, beta = pick(cum8), pick(beta8)
    last = cum[:, TOK - 1:]
    to_end = jnp.where(seg_row == seg_end, jnp.exp(last - cum), 0.0)
    through = jnp.where(seg_end == seg_prev, jnp.exp(last), 0.0)
    by_token = jnp.concatenate([cum, beta], axis=0).T
    in_first = seg_col == seg_prev

    xf[:HALO] = jnp.zeros((HALO, 1024), F32)
    for ref, lo, width in ((qx, 0, 256), (kx, 256, 256), (vx, 512, 512)):
        xf[HALO:, lo:lo + width] = ref[...].astype(F32)

    def activate(count):
        for w_ref, lo, width in ((cq_ref, 0, 256), (ck_ref, 256, 256), (cv_ref, 512, 512)):
            taps = w_ref[:, cols(c, width)]
            total = None
            for i in range(4):
                term = taps[i:i + 1] * xf[HALO - 3 + i:HALO - 3 + i + count, lo:lo + width]
                if i < 3:
                    term = term * keeps[3 - i][:count]
                total = term if total is None else total + term
            total = total * jax.nn.sigmoid(total)
            if lo < 512:
                for n in range(2):
                    head = total[:, n * DK:(n + 1) * DK]
                    norm = lax.rsqrt(jnp.sum(head * head, axis=-1, keepdims=True) + 1e-6)
                    act[:count, lo + n * DK:lo + (n + 1) * DK] = head * norm
            else:
                act[:count, lo:lo + width] = total

    activate(TOK)

    @pl.when(has_prev)
    def _():
        halo[0].wait_recv()

    xf[:HALO] = hx[...].astype(F32)
    activate(8)

    def lanes(size, height):
        where = lax.broadcasted_iota(jnp.int32, (height, 128), 1) // size
        return [(where == b).astype(BF16) for b in range(128 // size)]

    def expand(packed, size, masks, rows):
        zero = jnp.zeros((size, 128), BF16)
        out = []
        for b in range(TOK // size):
            src = rows(b)
            if src is None:
                out.append(jnp.concatenate([zero, zero], axis=1))
                continue
            half, inner = src * size // 128, src % (128 // size)
            piece = packed[:, halves[half]] * masks[inner]
            out.append(jnp.concatenate([piece, zero] if half == 0 else [zero, piece], axis=1))
        return jnp.concatenate(out, axis=0)

    def gather(low, size, masks, row_block, lane_block, count):
        both = []
        for half in range(2):
            total = None
            for p in range(count // 2):
                r, s = row_block(p), lane_block(p)
                piece = low[half, half][r * size:(r + 1) * size] * masks[s]
                total = piece if total is None else total + piece
            both.append(total)
        return jnp.concatenate(both, axis=1)

    every = range(OWN)
    kfs = [act[:, 256 + n * DK:256 + (n + 1) * DK] for n in range(2)]
    qfs = [act[:, n * DK:(n + 1) * DK] for n in range(2)]
    kbs = [kf.astype(BF16) for kf in kfs]
    k_ts = [kf.T for kf in kfs]
    k_tbs = [k_t.astype(BF16) for k_t in k_ts]
    grams = [dot(kbs[n], k_tbs[n]) for n in range(2)]
    cum_cols = [by_token[:, i:i + 1] for i in every]
    beta_cols = [by_token[:, OWN + i:OWN + i + 1] for i in every]
    start_cols = [jnp.where(in_first, jnp.exp(cum_cols[i]), 0.0) for i in every]

    pairs, lows = [], []
    for i in every:
        pair, low = {}, {}
        for r, s in quads:
            diff = cum_cols[i][halves[r]] - cum[i:i + 1, halves[s]]
            pair[r, s] = jnp.exp(jnp.where(same_doc[r, s], diff, -1e30))
            part = beta_cols[i][halves[r]] * grams[i // 2][halves[r], halves[s]] * pair[r, s]
            low[r, s] = (jnp.where(sub > lane, part, 0.0) if r == s else part).astype(BF16)
        pairs.append(pair)
        lows.append(low)

    m16 = lanes(16, 16)
    diag = lambda b: b
    eye16 = (lax.broadcasted_iota(jnp.int32, (16, TOK), 0) == lax.broadcasted_iota(jnp.int32, (16, TOK), 1) % 16).astype(F32)
    n1 = [-gather(lows[i], 16, m16, lambda p: p, lambda p: p, 16) for i in every]
    t = [eye16 + n1[i].astype(F32) for i in every]
    n2 = [dot(n1[i], expand(n1[i], 16, m16, diag)).astype(BF16) for i in every]
    power = n2
    for last_step in (False, False, True):
        wide = [expand(power[i], 16, m16, diag) for i in every]
        if last_step:
            t = [t[i] + dot(t[i].astype(BF16), wide[i]) for i in every]
        else:
            both = [dot(jnp.concatenate([power[i], t[i].astype(BF16)], axis=0), wide[i]) for i in every]
            power = [both[i][:16].astype(BF16) for i in every]
            t = [t[i] + both[i][16:] for i in every]

    for size in (16, 32, 64):
        masks = lanes(size, size)
        even = (lax.broadcasted_iota(jnp.int32, (size, TOK), 1) // size) % 2 == 0
        tb = [t[i].astype(BF16) for i in every]
        edge = [gather(lows[i], size, masks, lambda p: 2 * p + 1, lambda p: 2 * p, TOK // size // 2) for i in every]
        y = [dot(edge[i], expand(tb[i], size, masks, lambda b: b if b % 2 == 0 else None)).astype(BF16) for i in every]
        below = [dot(tb[i], expand(y[i], size, masks, lambda b: b - 1 if b % 2 else None)) for i in every]
        t = [jnp.concatenate([jnp.where(even, t[i], 0.0), jnp.where(even, -below[i], t[i])], axis=0) for i in every]

    rhs = []
    for i in every:
        v = act[:, 512 + i * DK:512 + (i + 1) * DK]
        rhs.append((beta_cols[i] * v, (beta_cols[i] * start_cols[i]) * kfs[i // 2]))
    tb = [t[i].astype(BF16) for i in every]
    rhs = [jnp.concatenate(rhs[i], axis=1) for i in every]
    uw_top = [dot(tb[i][:, :128], rhs[i][:128].astype(BF16)).astype(BF16) for i in every]
    rest = [(rhs[i][128:] - dot(lows[i][1, 0], uw_top[i])).astype(BF16) for i in every]
    uw = [jnp.concatenate([uw_top[i], dot(tb[i][:, 128:], rest[i]).astype(BF16)], axis=0) for i in every]
    kuw = [dot((k_ts[i // 2] * to_end[i:i + 1]).astype(BF16), uw[i]) for i in every]
    eye = (sub == lane).astype(F32)
    for i in every:
        mb[i, :, :DK] = (through[i:i + 1] * eye - kuw[i][:, DK:]).astype(BF16)
        mb[i, :, DK:] = kuw[i][:, :DK].astype(BF16)

    pl.semaphore_wait(told.at[3], 1)
    pl.semaphore_wait(told.at[4], 1)
    sends = []
    for i in every:
        owner = OWN * c + i
        sends.append((owner, pltpu.make_async_remote_copy(
            mb.at[i], rbuf.at[z], as_.at[i], ar.at[z], device_id={"ctx": at(owner)}, device_id_type=MESH,
        )))
    for owner, send in sends:
        @pl.when(z != owner)
        def _():
            send.start()

    @pl.when(own)
    def _():
        rbuf[z] = mb[head_at]

    scores = [dot(qfs[n].astype(BF16), k_tbs[n]) for n in range(2)]
    for i in every:
        inside = {q: (scores[i // 2][halves[q[0]], halves[q[1]]] * pairs[i][q]).astype(BF16) for q in quads}
        top = dot(inside[0, 0], uw_top[i])
        bottom = dot(jnp.concatenate([inside[1, 0], inside[1, 1]], axis=1), uw[i])
        q_start = qfs[i // 2] * start_cols[i]
        oloc[i, :128] = top[:, :DK]
        oloc[i, 128:] = bottom[:, :DK]
        qeff[i, :128] = (q_start[:128] - top[:, DK:]).astype(BF16)
        qeff[i, 128:] = (q_start[128:] - bottom[:, DK:]).astype(BF16)
    trade[5].wait_recv()
    gate = gx[...].astype(F32)
    gated[...] = gate * jax.nn.sigmoid(gate) * jnp.concatenate([gain_ref[...]] * OWN, axis=1)

    mine_at = jnp.where(own, head_at, 0)
    back = []
    for k in range(1, CHIPS):
        back.append(pltpu.make_async_remote_copy(
            sout.at[k], sbuf.at[mine_at], ss.at[k], sr.at[mine_at], device_id={"ctx": ring(k)}, device_id_type=MESH,
        ))
    ahead = pltpu.make_async_remote_copy(q8, s0buf, ys, yr, device_id={"ctx": up}, device_id_type=MESH)

    @pl.when(own)
    def _():
        for k in range(1, CHIPS):
            j = lax.rem(z + k, CHIPS)
            pltpu.make_async_remote_copy(
                mb.at[0], rbuf.at[j], as_.at[0], ar.at[j], device_id={"ctx": ring(k)}, device_id_type=MESH,
            ).wait_recv()

        def then(later, earlier):
            joined = dot(later[:, :DK], earlier)
            return jnp.concatenate([joined[:, :DK], joined[:, DK:] + later[:, DK:].astype(F32)], axis=1).astype(BF16)

        one = [rbuf[j] for j in range(CHIPS)]
        two = [then(one[2 * j + 1], one[2 * j]) for j in range(4)]
        four = [then(two[1], two[0]), then(two[3], two[2])]
        q8[...] = (dot(four[1][:, :DK], four[0][:, DK:]) + four[1][:, DK:].astype(F32)).astype(BF16)

        @pl.when(has_up)
        def _():
            ahead.start()

        six = then(two[2], four[0])
        start = jnp.concatenate([eye, jnp.zeros((DK, DK), F32)], axis=1).astype(BF16)
        for j, value in enumerate((
            start, one[0], two[0], then(one[2], two[0]), four[0], then(one[4], four[0]), six, then(one[6], six),
        )):
            pre[j] = value

        @pl.when(has_down)
        def _():
            ahead.wait_recv()

        s0 = s0buf[...]
        for k in (4, 3, 5, 2, 6, 1, 7, 0):
            step = pre[lax.rem(z + k, CHIPS)]
            state = (dot(step[:, :DK], s0) + step[:, DK:].astype(F32)).astype(BF16)
            if k:
                sout[k] = state
                back[k - 1].start()
            else:
                sbuf[head_at] = state

    for i in every:
        @pl.when(z != OWN * c + i)
        def _():
            pltpu.make_async_remote_copy(
                sout.at[0], sbuf.at[i], ss.at[0], sr.at[i], device_id={"ctx": partner}, device_id_type=MESH,
            ).wait_recv()
    theirs = pl.ds(pl.multiple_of(ROWS * (1 - c), 16), ROWS)
    swap = pltpu.make_async_remote_copy(
        mx.at[theirs], mixfull, ms, mr, device_id={"ctx": partner}, device_id_type=MESH,
    )
    for tokens in (theirs, mine):
        for i in every:
            o = oloc[i, tokens] + dot(qeff[i, tokens], sbuf[i])
            normed = o * lax.rsqrt(jnp.mean(o * o, axis=-1, keepdims=True) + 1e-6)
            mx[tokens, i * DK:(i + 1) * DK] = (normed * gated[tokens, i * DK:(i + 1) * DK]).astype(BF16)
        if tokens is theirs:
            swap.start()
    w_copy.wait()

    half = OWN * DK
    rows = lambda core: pl.ds(pl.multiple_of(core * half, 128), half)
    width = w_vm.shape[1] // 4
    mixed = mx[mine]
    order = (2, 1, 3, 0)
    for k in order:
        own_part[k] = dot(mixed, w_vm[rows(c), cols(lax.rem(x + k, n_x), width)])
    pl.semaphore_wait(told.at[2], 1)
    swap.wait_recv()
    mixed = mixfull[...]
    parts = []
    for k in order:
        to = lax.rem(x + k, n_x)
        part = (own_part[k] + dot(mixed, w_vm[rows(1 - c), cols(to, width)])).astype(BF16)
        if k == 0:
            total = part.astype(F32)
            continue
        sendp[k - 1] = part
        parts.append(pltpu.make_async_remote_copy(
            sendp.at[k - 1], recvp.at[k - 1], ps.at[k - 1], pr.at[k - 1], device_id={"head": to}, device_id_type=MESH,
        ))
        parts[-1].start()
    for part, k in zip(parts, order):
        part.wait_recv()
        total = total + recvp[k - 1].astype(F32)
    out_ref[...] = total.T.astype(BF16)

    for copy in trade + [swap] + parts:
        copy.wait_send()

    @pl.when(sends_halo)
    def _():
        for copy in halo:
            copy.wait_send()

    for owner, send in sends:
        @pl.when(z != owner)
        def _():
            send.wait_send()

    @pl.when(own & has_up)
    def _():
        ahead.wait_send()

    @pl.when(own)
    def _():
        for copy in back:
            copy.wait_send()


def body(
    query_in, key_in, value_in, gate_in, conv_query, conv_key, conv_value,
    decay_in, beta_in, norm_gain, doc_lengths, out_weight,
):
    anywhere, vmem = pl.BlockSpec(memory_space=pl.ANY), pl.BlockSpec(memory_space=pltpu.VMEM)
    dma = pltpu.SemaphoreType.DMA
    features = out_weight.shape[1] // 4
    return pl.pallas_call(
        kernel,
        out_shape=jax.ShapeDtypeStruct((features, ROWS), BF16),
        in_specs=[anywhere] * 7 + [vmem] * 5,
        out_specs=vmem,
        scratch_shapes=[
            pltpu.VMEM((TOK, 256), BF16),
            pltpu.VMEM((TOK, 256), BF16),
            pltpu.VMEM((TOK, 512), BF16),
            pltpu.VMEM((TOK, 512), BF16),
            pltpu.VMEM((2, 8, ROWS), F32),
            pltpu.VMEM((2, 8, ROWS), F32),
            pltpu.VMEM((2, HALO, 1024), BF16),
            pltpu.VMEM((HALO, 1024), BF16),
            pltpu.VMEM((HALO + TOK, 1024), F32),
            pltpu.VMEM((TOK, 1024), F32),
            pltpu.VMEM(out_weight.shape, BF16),
            pltpu.VMEM((OWN, DK, 2 * DK), BF16),
            pltpu.VMEM((OWN, TOK, DK), BF16),
            pltpu.VMEM((OWN, TOK, DK), F32),
            pltpu.VMEM((CHIPS, DK, 2 * DK), BF16),
            pltpu.VMEM((CHIPS, DK, 2 * DK), BF16),
            pltpu.VMEM((DK, DK), BF16),
            pltpu.VMEM((DK, DK), BF16),
            pltpu.VMEM((CHIPS, DK, DK), BF16),
            pltpu.VMEM((OWN, DK, DK), BF16),
            pltpu.VMEM((TOK, OWN * DK), F32),
            pltpu.VMEM((TOK, OWN * DK), BF16),
            pltpu.VMEM((ROWS, OWN * DK), BF16),
            pltpu.VMEM((4, ROWS, features), F32),
            pltpu.VMEM((3, ROWS, features), BF16),
            pltpu.VMEM((3, ROWS, features), BF16),
            dma((7,)), dma((6,)), dma((6,)), dma((2, 3)), dma((2,)), dma,
            dma((OWN,)), dma((CHIPS,)), dma, dma, dma((CHIPS,)), dma((OWN,)),
            dma, dma, dma((3,)), dma((3,)), pltpu.SemaphoreType.REGULAR((5,)),
        ],
        compiler_params=pltpu.CompilerParams(
            collective_id=0, has_side_effects=True, vmem_limit_bytes=56 << 20
        ),
        name="mixer",
    )(
        query_in, key_in, value_in, gate_in, decay_in, beta_in, out_weight,
        conv_query, conv_key, conv_value, doc_lengths.reshape(1, -1), norm_gain.reshape(1, -1),
    )


def solution(mesh):
    return jax.shard_map(
        body,
        mesh=mesh,
        in_specs=(
            P("ctx", "head"), P("ctx", "head"), P("ctx", "head"), P("ctx", "head"),
            P(None, "head"), P(None, "head"), P(None, "head"),
            P("head", "ctx"), P("head", "ctx"), P(), P(), P("head", None),
        ),
        out_specs=P("head", "ctx"),
        check_vma=False,
    )
```

time: 54.5 us -> 44.3 us (0.81)
  the two profiles are of different devices: /device:TPU:1 before, /device:TPU:24 now
where the time goes in v2:
time: 44.3 us; the launch traced here: 43.9 us
  Pallas kernels  42.3 us (95%)
  local copies, waits for them, and re-layouts  1.57 us (4%)
    pallas_call x1, Pallas kernels, body(): pl.pallas_call(kernel, out_shape=jax.ShapeDtypeStruct((features, ROWS), B...  42.3 us
    unnamed x1, local copies, waits for them, and re-layouts  1.57 us

profile of v2, /device:TPU:24, one launch (start us, length us, event | category | flops | bytes accessed | tf_op | source)
XLA Modules:
  0.0 43.9 jit_solution(8285866511610051301)
XLA Ops:
  0.0 42.3 %mixer.1 = bf16[512,128]{1,0:T(8,128)(2,1)} custom-call(bf16[128,512]{1,0:T(8,128)(2,1)} %q_hbm.1, bf16[128,512]{1,0:T(8,128)(2,1)} %k_hbm.1, bf16[128,1024]{1,0:T(8,128)(2,1)} %v_hbm.1, bf16[128,1024]{1,0:T(8,128)(2,1)} %g_hbm.1, f32[8,128]{1,0:T(8,128)} %dec_hbm.1, f32[8,128]{1,0:T(8,128)} %beta_hbm.1, bf16[1024,2048]{1,0:T(8,128)(2,1)} %w_hbm.1, ...), custom_call_target="tpu_custom_call" | custom-call | tf_op jit(solution)/shard_map/mixer/pallas_call | solution.py:469
  42.3 1.6 %copy.14 = bf16[512,128]{1,0:T(8,128)(2,1)} copy(bf16[512,128]{1,0:T(8,128)(2,1)} %mixer.1) | data formatting | bytes 262144

commit v3 on v2

--- a/solution.py
+++ b/solution.py
@@ -19,12 +19,17 @@
     return jnp.dot(a, b, preferred_element_type=F32)
 
 
+def fine_dot(a, b):
+    high = a.astype(BF16)
+    return dot(high, b) + dot((a - high.astype(F32)).astype(BF16), b)
+
+
 def kernel(
     q_hbm, k_hbm, v_hbm, g_hbm, dec_hbm, beta_hbm, w_hbm,
     cq_ref, ck_ref, cv_ref, docs_ref, gain_ref,
     out_ref,
     qx, kx, vx, gx, dx, bx, hb, hx, xf, act, w_vm,
-    mb, qeff, oloc, rbuf, pre, q8, s0buf, sout, sbuf, gated, mx, mixfull, own_part, sendp, recvp,
+    mb, qeff, oloc, rbuf, pre, q8, s0buf, sout, sbuf, gated, mx, mixfull, own_part, sendp, via, joined, recvp,
     lsem, xs, xr, hl, hs, hr, as_, ar, ys, yr, ss, sr, ms, mr, ps, pr, told,
 ):
     ctx, x = lax.axis_index("ctx"), lax.axis_index("head")
@@ -139,7 +144,6 @@
 
     signal(told.at[0], ctx=ring(1))
     signal(told.at[1], ctx=ring(-1))
-    signal(told.at[2], head=x_next)
 
     first = chip * TOK
     sub = lax.broadcasted_iota(jnp.int32, (128, 128), 0)
@@ -166,15 +170,10 @@
         same = seg_col[halves[r]] == seg_row[:, halves[s]]
         same_doc[r, s] = same & (sub >= lane) if r == s else same
 
-    for copy in local:
+    for copy in local[4:]:
         copy.wait()
-    for copy in trade[:5]:
+    for copy in trade[:2]:
         copy.wait_recv()
-
-    pl.semaphore_wait(told.at[0], 1)
-    pl.semaphore_wait(told.at[1], 1)
-    signal(told.at[3], ctx=ring(2))
-    signal(told.at[4], ctx=ring(-2))
 
     decay = jnp.concatenate([dx[0], dx[1]], axis=1)
     log_gamma = -jax.nn.softplus(decay)
@@ -187,6 +186,16 @@
     through = jnp.where(seg_end == seg_prev, jnp.exp(last), 0.0)
     by_token = jnp.concatenate([cum, beta], axis=0).T
     in_first = seg_col == seg_prev
+
+    pl.semaphore_wait(told.at[0], 1)
+    pl.semaphore_wait(told.at[1], 1)
+    signal(told.at[2], ctx=ring(2))
+    signal(told.at[3], ctx=ring(-2))
+
+    for copy in local[:4]:
+        copy.wait()
+    for copy in trade[2:5]:
+        copy.wait_recv()
 
     xf[:HALO] = jnp.zeros((HALO, 1024), F32)
     for ref, lo, width in ((qx, 0, 256), (kx, 256, 256), (vx, 512, 512)):
@@ -303,14 +312,14 @@
     uw_top = [dot(tb[i][:, :128], rhs[i][:128].astype(BF16)).astype(BF16) for i in every]
     rest = [(rhs[i][128:] - dot(lows[i][1, 0], uw_top[i])).astype(BF16) for i in every]
     uw = [jnp.concatenate([uw_top[i], dot(tb[i][:, 128:], rest[i]).astype(BF16)], axis=0) for i in every]
-    kuw = [dot((k_ts[i // 2] * to_end[i:i + 1]).astype(BF16), uw[i]) for i in every]
+    kuw = [fine_dot(k_ts[i // 2] * to_end[i:i + 1], uw[i]) for i in every]
     eye = (sub == lane).astype(F32)
     for i in every:
         mb[i, :, :DK] = (through[i:i + 1] * eye - kuw[i][:, DK:]).astype(BF16)
         mb[i, :, DK:] = kuw[i][:, :DK].astype(BF16)
 
+    pl.semaphore_wait(told.at[2], 1)
     pl.semaphore_wait(told.at[3], 1)
-    pl.semaphore_wait(told.at[4], 1)
     sends = []
     for i in every:
         owner = OWN * c + i
@@ -328,9 +337,9 @@
 
     scores = [dot(qfs[n].astype(BF16), k_tbs[n]) for n in range(2)]
     for i in every:
-        inside = {q: (scores[i // 2][halves[q[0]], halves[q[1]]] * pairs[i][q]).astype(BF16) for q in quads}
-        top = dot(inside[0, 0], uw_top[i])
-        bottom = dot(jnp.concatenate([inside[1, 0], inside[1, 1]], axis=1), uw[i])
+        inside = {q: scores[i // 2][halves[q[0]], halves[q[1]]] * pairs[i][q] for q in quads}
+        top = fine_dot(inside[0, 0], uw_top[i])
+        bottom = fine_dot(jnp.concatenate([inside[1, 0], inside[1, 1]], axis=1), uw[i])
         q_start = qfs[i // 2] * start_cols[i]
         oloc[i, :128] = top[:, :DK]
         oloc[i, 128:] = bottom[:, :DK]
@@ -416,27 +425,41 @@
     order = (2, 1, 3, 0)
     for k in order:
         own_part[k] = dot(mixed, w_vm[rows(c), cols(lax.rem(x + k, n_x), width)])
-    pl.semaphore_wait(told.at[2], 1)
     swap.wait_recv()
     mixed = mixfull[...]
-    parts = []
-    for k in order:
-        to = lax.rem(x + k, n_x)
-        part = (own_part[k] + dot(mixed, w_vm[rows(1 - c), cols(to, width)])).astype(BF16)
-        if k == 0:
-            total = part.astype(F32)
-            continue
-        sendp[k - 1] = part
-        parts.append(pltpu.make_async_remote_copy(
-            sendp.at[k - 1], recvp.at[k - 1], ps.at[k - 1], pr.at[k - 1], device_id={"head": to}, device_id_type=MESH,
+
+    def part(k):
+        block = cols(lax.rem(x + k, n_x), width)
+        return (own_part[k] + dot(mixed, w_vm[rows(1 - c), block])).astype(BF16)
+
+    sent = []
+
+    def pass_on(n, src, dst, to):
+        sent.append(pltpu.make_async_remote_copy(
+            src, dst, ps.at[n], pr.at[n], device_id={"head": to}, device_id_type=MESH,
         ))
-        parts[-1].start()
-    for part, k in zip(parts, order):
-        part.wait_recv()
-        total = total + recvp[k - 1].astype(F32)
-    out_ref[...] = total.T.astype(BF16)
-
-    for copy in trade + [swap] + parts:
+        sent[-1].start()
+
+    early, late = pl.ds(0, ROWS // 2), pl.ds(ROWS // 2, ROWS // 2)
+    sendp[1] = part(2)
+    pass_on(0, sendp.at[1, early], via.at[0], x_next)
+    pass_on(1, sendp.at[1, late], via.at[1], x_prev)
+    sendp[0] = part(1)
+    pass_on(2, sendp.at[0, late], recvp.at[0, late], x_next)
+    sendp[2] = part(3)
+    pass_on(3, sendp.at[2, early], recvp.at[1, early], x_prev)
+    total = part(0).astype(F32)
+    sent[0].wait_recv()
+    joined[0] = (sendp[0, early].astype(F32) + via[0].astype(F32)).astype(BF16)
+    pass_on(4, joined.at[0], recvp.at[0, early], x_next)
+    sent[1].wait_recv()
+    joined[1] = (sendp[2, late].astype(F32) + via[1].astype(F32)).astype(BF16)
+    pass_on(5, joined.at[1], recvp.at[1, late], x_prev)
+    for copy in sent[2:]:
+        copy.wait_recv()
+    out_ref[...] = (total + recvp[0].astype(F32) + recvp[1].astype(F32)).T.astype(BF16)
+
+    for copy in trade + [swap] + sent:
         copy.wait_send()
 
     @pl.when(sends_halo)
@@ -497,10 +520,12 @@
             pltpu.VMEM((ROWS, OWN * DK), BF16),
             pltpu.VMEM((4, ROWS, features), F32),
             pltpu.VMEM((3, ROWS, features), BF16),
-            pltpu.VMEM((3, ROWS, features), BF16),
+            pltpu.VMEM((2, ROWS // 2, features), BF16),
+            pltpu.VMEM((2, ROWS // 2, features), BF16),
+            pltpu.VMEM((2, ROWS, features), BF16),
             dma((7,)), dma((6,)), dma((6,)), dma((2, 3)), dma((2,)), dma,
             dma((OWN,)), dma((CHIPS,)), dma, dma, dma((CHIPS,)), dma((OWN,)),
-            dma, dma, dma((3,)), dma((3,)), pltpu.SemaphoreType.REGULAR((5,)),
+            dma, dma, dma((6,)), dma((6,)), pltpu.SemaphoreType.REGULAR((4,)),
         ],
         compiler_params=pltpu.CompilerParams(
             collective_id=0, has_side_effects=True, vmem_limit_bytes=56 << 20

time: 44.3 us -> 42.9 us (0.968)
  Pallas kernels: 42.3 us -> 41.2 us
    pallas_call x1, Pallas kernels: 42.3 us -> 41.2 us  [body(): pl.pallas_call(kernel, out_shape=jax.ShapeDtypeStruct((features, ROWS), B...]
where the time goes in v3:
time: 42.9 us; the launch traced here: 42.8 us
  Pallas kernels  41.2 us (96%)
  local copies, waits for them, and re-layouts  1.57 us (4%)
    pallas_call x1, Pallas kernels, body(): pl.pallas_call(kernel, out_shape=jax.ShapeDtypeStruct((features, ROWS), B...  41.2 us
    unnamed x1, local copies, waits for them, and re-layouts  1.57 us

profile of v3, /device:TPU:24, one launch (start us, length us, event | category | flops | bytes accessed | tf_op | source)
XLA Modules:
  0.0 42.8 jit_solution(18009373458657552557)
XLA Ops:
  0.0 41.2 %mixer.1 = bf16[512,128]{1,0:T(8,128)(2,1)} custom-call(bf16[128,512]{1,0:T(8,128)(2,1)} %q_hbm.1, bf16[128,512]{1,0:T(8,128)(2,1)} %k_hbm.1, bf16[128,1024]{1,0:T(8,128)(2,1)} %v_hbm.1, bf16[128,1024]{1,0:T(8,128)(2,1)} %g_hbm.1, f32[8,128]{1,0:T(8,128)} %dec_hbm.1, f32[8,128]{1,0:T(8,128)} %beta_hbm.1, bf16[1024,2048]{1,0:T(8,128)(2,1)} %w_hbm.1, ...), custom_call_target="tpu_custom_call" | custom-call | tf_op jit(solution)/shard_map/mixer/pallas_call | solution.py:492
  41.2 1.6 %copy.14 = bf16[512,128]{1,0:T(8,128)(2,1)} copy(bf16[512,128]{1,0:T(8,128)(2,1)} %mixer.1) | data formatting | bytes 262144

commit v4 on v3

--- a/solution.py
+++ b/solution.py
@@ -186,6 +186,21 @@
     through = jnp.where(seg_end == seg_prev, jnp.exp(last), 0.0)
     by_token = jnp.concatenate([cum, beta], axis=0).T
     in_first = seg_col == seg_prev
+    every = range(OWN)
+    cum_cols = [by_token[:, i:i + 1] for i in every]
+    beta_cols = [by_token[:, OWN + i:OWN + i + 1] for i in every]
+    start_cols = [jnp.where(in_first, jnp.exp(cum_cols[i]), 0.0) for i in every]
+    pairs, writes = [], []
+    for i in every:
+        pair, write = {}, {}
+        for r, s in quads:
+            diff = cum_cols[i][halves[r]] - cum[i:i + 1, halves[s]]
+            pair[r, s] = jnp.exp(jnp.where(same_doc[r, s], diff, -1e30))
+            write[r, s] = beta_cols[i][halves[r]] * pair[r, s]
+            if r == s:
+                write[r, s] = jnp.where(sub > lane, write[r, s], 0.0)
+        pairs.append(pair)
+        writes.append(write)
 
     pl.semaphore_wait(told.at[0], 1)
     pl.semaphore_wait(told.at[1], 1)
@@ -201,8 +216,8 @@
     for ref, lo, width in ((qx, 0, 256), (kx, 256, 256), (vx, 512, 512)):
         xf[HALO:, lo:lo + width] = ref[...].astype(F32)
 
-    def activate(count):
-        for w_ref, lo, width in ((cq_ref, 0, 256), (ck_ref, 256, 256), (cv_ref, 512, 512)):
+    def activate(count, *parts):
+        for w_ref, lo, width in parts:
             taps = w_ref[:, cols(c, width)]
             total = None
             for i in range(4):
@@ -219,14 +234,15 @@
             else:
                 act[:count, lo:lo + width] = total
 
-    activate(TOK)
+    of_q, of_k, of_v = (cq_ref, 0, 256), (ck_ref, 256, 256), (cv_ref, 512, 512)
+    activate(TOK, of_k, of_v)
 
     @pl.when(has_prev)
     def _():
         halo[0].wait_recv()
 
     xf[:HALO] = hx[...].astype(F32)
-    activate(8)
+    activate(8, of_k, of_v)
 
     def lanes(size, height):
         where = lax.broadcasted_iota(jnp.int32, (height, 128), 1) // size
@@ -256,26 +272,16 @@
             both.append(total)
         return jnp.concatenate(both, axis=1)
 
-    every = range(OWN)
     kfs = [act[:, 256 + n * DK:256 + (n + 1) * DK] for n in range(2)]
-    qfs = [act[:, n * DK:(n + 1) * DK] for n in range(2)]
     kbs = [kf.astype(BF16) for kf in kfs]
     k_ts = [kf.T for kf in kfs]
     k_tbs = [k_t.astype(BF16) for k_t in k_ts]
     grams = [dot(kbs[n], k_tbs[n]) for n in range(2)]
-    cum_cols = [by_token[:, i:i + 1] for i in every]
-    beta_cols = [by_token[:, OWN + i:OWN + i + 1] for i in every]
-    start_cols = [jnp.where(in_first, jnp.exp(cum_cols[i]), 0.0) for i in every]
-
-    pairs, lows = [], []
-    for i in every:
-        pair, low = {}, {}
+    lows = []
+    for i in every:
+        low = {}
         for r, s in quads:
-            diff = cum_cols[i][halves[r]] - cum[i:i + 1, halves[s]]
-            pair[r, s] = jnp.exp(jnp.where(same_doc[r, s], diff, -1e30))
-            part = beta_cols[i][halves[r]] * grams[i // 2][halves[r], halves[s]] * pair[r, s]
-            low[r, s] = (jnp.where(sub > lane, part, 0.0) if r == s else part).astype(BF16)
-        pairs.append(pair)
+            low[r, s] = (grams[i // 2][halves[r], halves[s]] * writes[i][r, s]).astype(BF16)
         lows.append(low)
 
     m16 = lanes(16, 16)
@@ -335,6 +341,8 @@
     def _():
         rbuf[z] = mb[head_at]
 
+    activate(TOK, of_q)
+    qfs = [act[:, n * DK:(n + 1) * DK] for n in range(2)]
     scores = [dot(qfs[n].astype(BF16), k_tbs[n]) for n in range(2)]
     for i in every:
         inside = {q: scores[i // 2][halves[q[0]], halves[q[1]]] * pairs[i][q] for q in quads}
@@ -440,22 +448,23 @@
         ))
         sent[-1].start()
 
+    piece = ROWS // 4
+    rows_of = [pl.ds(n * piece, piece) for n in range(4)]
     early, late = pl.ds(0, ROWS // 2), pl.ds(ROWS // 2, ROWS // 2)
     sendp[1] = part(2)
-    pass_on(0, sendp.at[1, early], via.at[0], x_next)
-    pass_on(1, sendp.at[1, late], via.at[1], x_prev)
+    for n in (0, 2, 1, 3):
+        pass_on(n, sendp.at[1, rows_of[n]], via.at[n], x_next if n < 2 else x_prev)
     sendp[0] = part(1)
-    pass_on(2, sendp.at[0, late], recvp.at[0, late], x_next)
+    pass_on(4, sendp.at[0, late], recvp.at[0, late], x_next)
     sendp[2] = part(3)
-    pass_on(3, sendp.at[2, early], recvp.at[1, early], x_prev)
+    pass_on(5, sendp.at[2, early], recvp.at[1, early], x_prev)
     total = part(0).astype(F32)
-    sent[0].wait_recv()
-    joined[0] = (sendp[0, early].astype(F32) + via[0].astype(F32)).astype(BF16)
-    pass_on(4, joined.at[0], recvp.at[0, early], x_next)
-    sent[1].wait_recv()
-    joined[1] = (sendp[2, late].astype(F32) + via[1].astype(F32)).astype(BF16)
-    pass_on(5, joined.at[1], recvp.at[1, late], x_prev)
-    for copy in sent[2:]:
+    for at_sent, n in enumerate((0, 2, 1, 3)):
+        side = 0 if n < 2 else 1
+        sent[at_sent].wait_recv()
+        joined[n] = (sendp[2 * side, rows_of[n]].astype(F32) + via[n].astype(F32)).astype(BF16)
+        pass_on(6 + n, joined.at[n], recvp.at[side, rows_of[n]], x_prev if side else x_next)
+    for copy in sent[4:]:
         copy.wait_recv()
     out_ref[...] = (total + recvp[0].astype(F32) + recvp[1].astype(F32)).T.astype(BF16)
 
@@ -520,12 +529,12 @@
             pltpu.VMEM((ROWS, OWN * DK), BF16),
             pltpu.VMEM((4, ROWS, features), F32),
             pltpu.VMEM((3, ROWS, features), BF16),
-            pltpu.VMEM((2, ROWS // 2, features), BF16),
-            pltpu.VMEM((2, ROWS // 2, features), BF16),
+            pltpu.VMEM((4, ROWS // 4, features), BF16),
+            pltpu.VMEM((4, ROWS // 4, features), BF16),
             pltpu.VMEM((2, ROWS, features), BF16),
             dma((7,)), dma((6,)), dma((6,)), dma((2, 3)), dma((2,)), dma,
             dma((OWN,)), dma((CHIPS,)), dma, dma, dma((CHIPS,)), dma((OWN,)),
-            dma, dma, dma((6,)), dma((6,)), pltpu.SemaphoreType.REGULAR((4,)),
+            dma, dma, dma((10,)), dma((10,)), pltpu.SemaphoreType.REGULAR((4,)),
         ],
         compiler_params=pltpu.CompilerParams(
             collective_id=0, has_side_effects=True, vmem_limit_bytes=56 << 20

time: 42.9 us -> 42.4 us (0.988)
  Pallas kernels: 41.2 us -> 40.7 us
    pallas_call x1, Pallas kernels: 41.2 us -> 40.7 us  [body(): pl.pallas_call(kernel, out_shape=jax.ShapeDtypeStruct((features, ROWS), B...]
where the time goes in v4:
time: 42.4 us; the launch traced here: 42.3 us
  Pallas kernels  40.7 us (96%)
  local copies, waits for them, and re-layouts  1.57 us (4%)
    pallas_call x1, Pallas kernels, body(): pl.pallas_call(kernel, out_shape=jax.ShapeDtypeStruct((features, ROWS), B...  40.7 us
    unnamed x1, local copies, waits for them, and re-layouts  1.57 us

profile of v4, /device:TPU:24, one launch (start us, length us, event | category | flops | bytes accessed | tf_op | source)
XLA Modules:
  0.0 42.3 jit_solution(448055810694293915)
XLA Ops:
  0.0 40.7 %mixer.1 = bf16[512,128]{1,0:T(8,128)(2,1)} custom-call(bf16[128,512]{1,0:T(8,128)(2,1)} %q_hbm.1, bf16[128,512]{1,0:T(8,128)(2,1)} %k_hbm.1, bf16[128,1024]{1,0:T(8,128)(2,1)} %v_hbm.1, bf16[128,1024]{1,0:T(8,128)(2,1)} %g_hbm.1, f32[8,128]{1,0:T(8,128)} %dec_hbm.1, f32[8,128]{1,0:T(8,128)} %beta_hbm.1, bf16[1024,2048]{1,0:T(8,128)(2,1)} %w_hbm.1, ...), custom_call_target="tpu_custom_call" | custom-call | tf_op jit(solution)/shard_map/mixer/pallas_call | solution.py:501
  40.7 1.6 %copy.14 = bf16[512,128]{1,0:T(8,128)(2,1)} copy(bf16[512,128]{1,0:T(8,128)(2,1)} %mixer.1) | data formatting | bytes 262144
